TPU v7x, 32 devices: a whole 2x2x4 slice. The times are simulated.
32 devices in a mesh: row: 4 (over y, x), col: 8 (over z, core).
Axes of the slice: x: 2, y: 2, z: 4, core: 2. Of those that a mesh axis runs over, the one named last changes fastest.
Arguments:
- matrix: float32 [6, 4, 128, 128, 8, 128], P(None, 'row', None, None, 'col'), may hold values from -6 to 6
- factors: float32 [10, 512, 512], P(None, None, 'col'), as said below
- starts: int32 [10], replicated, may hold values from 0 to 2560, as said below
Outputs:
- updated: float32 [6, 4, 128, 128, 8, 128], P(None, 'row', None, None, 'col')
Inputs may be any that keep to these rules, and one draw needn't show every extreme that they name: starts[w] = starts[0] + 256 * w, and starts[0] is a multiple of 128. Each factors[w] is orthogonal.
All inputs are finite; a program needn't handle non-finite values.
Results may differ from a plain program's by a relative error of at most 0.0001.
Values sent between devices are 32-bit elements; how exact they have to be, the bound alone decides.
No kernel may reach another device: no remote copies, remote signals or barrier semaphores. Data moves between devices by JAX's collectives and lax.ppermute only.
A program may use at most 384 MiB of HBM per device.

v0:
```python
import jax
import jax.numpy as jnp
from jax import lax
from jax.sharding import PartitionSpec as P

WIN = 512
SHIFT = 256
WINS = 10


def pick_tiles(first_tile, per_device, axis_count, position, span_tiles):
    global_tiles = (
        first_tile
        + jnp.remainder(position - first_tile, axis_count)
        + jnp.arange(per_device, dtype=jnp.int32) * axis_count
    )
    tile_valid = global_tiles < first_tile + span_tiles
    return (tile_valid, jnp.where(tile_valid, global_tiles // axis_count, 0))


def band_order(first_tile, axis_count, per_device, span_tiles):
    places = jnp.arange(span_tiles, dtype=jnp.int32)
    return jnp.remainder(first_tile + places, axis_count) * per_device + places // axis_count


def slot_order(first_tile, axis_count, per_device, span_tiles):
    slot_ids = jnp.arange(axis_count * per_device, dtype=jnp.int32)
    places = (
        jnp.remainder(slot_ids // per_device - first_tile, axis_count)
        + slot_ids % per_device * axis_count
    )
    slot_valid = places < span_tiles
    return (slot_valid, jnp.where(slot_valid, places, 0))


def body(matrix, factors, starts):
    row_count = lax.axis_size("row")
    col_count = lax.axis_size("col")
    row_place = lax.axis_index("row")
    col_place = lax.axis_index("col")
    row_cycles = matrix.shape[0]
    tile_size = matrix.shape[2]
    col_cycles = matrix.shape[3]
    span_tiles = (WIN + SHIFT * (WINS - 1)) // tile_size
    first_tile = starts[0] // tile_size
    all_factors = lax.all_gather(factors, "col", axis=2, tiled=True)

    def left_step(window, band_rows):
        offset_row = starts[window] - starts[0]
        factor_now = lax.dynamic_index_in_dim(all_factors, window, 0, keepdims=False)
        window_rows = lax.dynamic_slice_in_dim(band_rows, offset_row, WIN, 0)
        result_rows = jnp.dot(
            factor_now.T,
            window_rows,
            precision=lax.Precision.HIGHEST,
            preferred_element_type=jnp.float32,
        )
        return lax.dynamic_update_slice_in_dim(band_rows, result_rows, offset_row, 0)

    def right_step(window, band_cols):
        offset_col = starts[window] - starts[0]
        factor_now = lax.dynamic_index_in_dim(all_factors, window, 0, keepdims=False)
        window_cols = lax.dynamic_slice_in_dim(band_cols, offset_col, WIN, 1)
        result_cols = jnp.dot(
            window_cols,
            factor_now,
            precision=lax.Precision.HIGHEST,
            preferred_element_type=jnp.float32,
        )
        return lax.dynamic_update_slice_in_dim(band_cols, result_cols, offset_col, 1)

    local_tiles = matrix.reshape(row_cycles, tile_size, col_cycles * tile_size)
    rows_each = -(-span_tiles // row_count)
    row_valid, row_index = pick_tiles(first_tile, rows_each, row_count, row_place, span_tiles)
    picked = jnp.where(row_valid[:, None, None], jnp.take(local_tiles, row_index, axis=0), 0.0)
    received = lax.all_to_all(picked, "row", split_axis=2, concat_axis=0, tiled=True)
    band_rows = jnp.take(received, band_order(first_tile, row_count, rows_each, span_tiles), axis=0)
    band_rows = band_rows.reshape(span_tiles * tile_size, received.shape[2])
    band_rows = lax.fori_loop(0, WINS, left_step, band_rows)
    row_tiles = band_rows.reshape(span_tiles, tile_size, received.shape[2])
    send_valid, send_place = slot_order(first_tile, row_count, rows_each, span_tiles)
    backsend = jnp.where(send_valid[:, None, None], jnp.take(row_tiles, send_place, axis=0), 0.0)
    returned = lax.all_to_all(backsend, "row", split_axis=0, concat_axis=2, tiled=True)
    for member in range(rows_each):
        local_tiles = jnp.where(
            row_valid[member],
            lax.dynamic_update_index_in_dim(local_tiles, returned[member], row_index[member], 0),
            local_tiles,
        )
    local_rows = row_cycles * tile_size
    column_view = local_tiles.reshape(local_rows, col_cycles, tile_size)
    cols_each = -(-span_tiles // col_count)
    col_valid, col_index = pick_tiles(first_tile, cols_each, col_count, col_place, span_tiles)
    picked_cols = jnp.where(col_valid[None, :, None], jnp.take(column_view, col_index, axis=1), 0.0)
    col_order = band_order(first_tile, col_count, cols_each, span_tiles)
    received_cols = lax.all_to_all(picked_cols, "col", split_axis=0, concat_axis=1, tiled=True)
    share_rows = received_cols.shape[0]
    band_cols = jnp.take(received_cols, col_order, axis=1).reshape(
        share_rows, span_tiles * tile_size
    )
    band_cols = lax.fori_loop(0, WINS, right_step, band_cols)
    slot_valid, slot_place = slot_order(first_tile, col_count, cols_each, span_tiles)
    send_cols = jnp.where(
        slot_valid[None, :, None],
        jnp.take(band_cols.reshape(share_rows, span_tiles, tile_size), slot_place, axis=1),
        0.0,
    )
    returned_cols = lax.all_to_all(send_cols, "col", split_axis=1, concat_axis=0, tiled=True)
    for member in range(cols_each):
        column_view = jnp.where(
            col_valid[member],
            lax.dynamic_update_index_in_dim(
                column_view, returned_cols[:, member], col_index[member], 1
            ),
            column_view,
        )
    return column_view.reshape(matrix.shape)


def solution(mesh):
    placed = (P(None, "row", None, None, "col", None), P(None, None, "col"), P())
    return jax.shard_map(
        body,
        mesh=mesh,
        in_specs=placed,
        out_specs=P(None, "row", None, None, "col", None),
        check_vma=False,
    )
```

profile of v0, /device:TPU:2, one launch (start us, length us, event | category | flops | bytes accessed | tf_op | source)
XLA Modules:
  0.0 2669.3 jit_solution(13656926926000482717)
XLA Ops:
  9.7 133.3 %reduce.3 = f32[6,128,128,128]{3,2,1,0:T(8,128)} reduce(f32[6,1,128,128,1,128]{5,4,3,2,1,0:T(1,128)} %param.7, f32[]{:T(128)} %broadcast.1276), dimensions={1,4}, to_apply=%param.7.reduce_sub_computation.3 | reduce | bytes 100663296 | tf_op args[0]
  143.0 53.6 %reshape.633 = f32[6,128,16384]{2,1,0:T(8,128)} reshape(f32[6,128,128,128]{3,2,1,0:T(8,128)} %reduce.3) | data formatting | bytes 100663296 | tf_op jit(solution)/shard_map/reshape | solution.py:72
  196.6 22.3 fusion.49
  273.7 34.3 %fusion.10 = f32[6,128,16384]{2,1,0:T(8,128)} fusion(f32[6,128,5376]{2,1,0:T(8,128)} %gather_fusion.7, f32[6,128,5504]{2,1,0:T(8,128)} %gather_fusion.6, f32[6,128,5504]{2,1,0:T(8,128)} %gather_fusion.5, pred[6]{0:T(512)(128)(4,1)S(1)} %get-tuple-element.199, pred[6]{0:T(512)(128)(4,1)S(1)} %get-tuple-element.236), kind=kLoop, calls=%fused_computation.19 | loop fusion | flops 50331648 | bytes 100663312 | tf_op jit(solution)/shard_map/jit(_where)/select_n | solution.py:75
  308.0 58.4 %copy.74 = f32[6,128,16384]{1,0,2:T(8,128)} copy(f32[6,128,16384]{2,1,0:T(8,128)} %fusion.10) | data formatting | bytes 100663296 | tf_op jit(solution)/shard_map/jit(_where)/select_n | solution.py:75
  380.9 102.0 %all-gather.2.cloned.1.call-done = f32[10,512,512]{1,2,0:T(8,128)} async-done(((f32[10,512,64]{1,2,0:T(8,128)}), f32[10,512,512]{1,2,0:T(8,128)}) %all-gather.2.cloned.1.call-update) | async-done | bytes 10485776 | tf_op jit(solution)/shard_map/all_gather | solution.py:46
  494.1 606.8 %all-to-all-done = f32[6,128,16384]{1,0,2:T(8,128)} async-done(((f32[6,128,16384]{1,0,2:T(8,128)}), f32[6,128,16384]{1,0,2:T(8,128)}, u32[]{:S(2)}, u32[]{:S(2)}) %all-to-all-start) | async-done | bytes 50331680 | tf_op jit(solution)/shard_map/all_to_all | solution.py:76
  1100.9 58.1 %copy.76 = f32[4,6,128,4096]{3,2,1,0:T(8,128)} copy(f32[4,6,128,4096]{2,1,3,0:T(8,128)} %bitcast.10) | data formatting | bytes 100663296 | tf_op jit(solution)/shard_map/all_to_all | solution.py:76
  1159.1 32.2 %gather_fusion = f32[22,128,4096]{2,1,0:T(8,128)} fusion(f32[24,128,4096]{2,1,0:T(8,128)} %bitcast.115, s32[1024]{0:T(1024)S(1)} %pad_clamp_fusion.4), kind=kCustom, calls=%fused_computation | custom fusion | bytes 92274776 | tf_op jit(solution)/shard_map/jit(_take)/gather | solution.py:77
  1191.3 34.3 %bitcast_select_fusion = f32[2816,4096]{1,0:T(8,128)} fusion(f32[22,128,4096]{2,1,0:T(8,128)} %gather_fusion, pred[2816]{0:T(1024)(128)(4,1)S(1)} %broadcast_bitcast_fusion.1), kind=kLoop, calls=%fused_computation.21 | loop fusion | flops 11534336 | bytes 92277504 | tf_op jit(solution)/shard_map/jit(_take)/select_n | solution.py:77
  1225.5 415.1 %while.26 = (s32[]{:T(128)}, f32[2816,4096]{1,0:T(8,128)}, f32[10,512,512]{2,1,0:T(8,128)}, s32[10]{0:T(128)S(1)}, s32[]{:T(128)}, /*index=5*/s32[]{:T(128)}, s32[]{:T(128)}) while((s32[]{:T(128)}, f32[2816,4096]{1,0:T(8,128)}, f32[10,512,512]{2,1,0:T(8,128)}, s32[10]{0:T(128)S(1)}, s32[]{:T(128)}, /*index=5*/s32[]{:T(128)}, s32[]{:T(128)}) %tuple.96), condition=%wide.region_1.2_spmd, body=%wide.region_0.1_spmd.sunk | while | flops 12884901888 | bytes 34603672 | solution.py:79
  1244.8 22.3 dynamic_update_slice.27
  1286.4 22.3 dynamic_update_slice.27
  1328.0 22.2 dynamic_update_slice.27
  1369.5 22.3 dynamic_update_slice.27
  1393.7 17.4 fusion.67
  1411.1 22.2 dynamic_update_slice.27
  1452.7 22.3 dynamic_update_slice.27
  1494.3 22.2 dynamic_update_slice.27
  1518.5 17.4 fusion.67
  1535.9 22.3 dynamic_update_slice.27
  1577.5 22.2 dynamic_update_slice.27
  1619.0 21.7 dynamic_update_slice.27
  1640.7 35.0 %gather_fusion.1 = f32[24,128,4096]{2,1,0:T(8,128)} fusion(f32[22,128,4096]{2,1,0:T(8,128)} %bitcast.111, s32[1024]{0:T(1024)S(1)} %pad_clamp_fusion.3), kind=kCustom, calls=%fused_computation.1 | custom fusion | bytes 100663392 | tf_op jit(solution)/shard_map/jit(_take)/gather | solution.py:82
  1675.7 35.7 %select_select_fusion = f32[24,128,4096]{2,1,0:T(8,128)} fusion(f32[24,128,4096]{2,1,0:T(8,128)} %gather_fusion.1, pred[24]{0:T(512)(128)(4,1)S(1)} %copy-done.8, pred[24]{0:T(512)(128)(4,1)S(1)} %copy-done.9), kind=kLoop, calls=%fused_computation.20 | loop fusion | flops 25165824 | bytes 100663344 | tf_op jit(solution)/shard_map/jit(_where)/select_n | solution.py:82
  1738.0 527.0 %all-to-all-done.1 = f32[24,128,4096]{2,1,0:T(8,128)} async-done(((f32[24,128,4096]{2,1,0:T(8,128)}), f32[24,128,4096]{2,1,0:T(8,128)}, u32[]{:S(2)}, u32[]{:S(2)}) %all-to-all-start.1) | async-done | bytes 50331680 | tf_op jit(solution)/shard_map/all_to_all | solution.py:83
  2265.0 33.1 %slice_bitcast_fusion = (f32[4,1,16,8,4096]{4,3,2,1,0:T(8,128)}, f32[4,1,16,8,4096]{4,3,2,1,0:T(8,128)}, f32[4,1,16,8,4096]{4,3,2,1,0:T(8,128)}, f32[4,1,16,8,40...) fusion(f32[6,128,4,4096]{3,1,0,2:T(8,128)} %bitcast.17), kind=kLoop, calls=%fused_computation.22 | loop fusion | bytes 100663296
  2395.8 41.2 %copy.102 = f32[96,8,128,128]{3,2,1,0:T(8,128)} copy(f32[96,8,128,128]{3,1,2,0:T(8,128)} %bitcast.110) | data formatting | bytes 100663296
  2437.1 46.1 %copy.84 = f32[768,128,128]{2,0,1:T(8,128)} copy(f32[768,128,128]{2,1,0:T(8,128)} %bitcast.112) | data formatting | bytes 100663296 | tf_op jit(solution)/shard_map/reshape | solution.py:91
  2492.5 37.6 %all-to-all-done.2 = f32[768,3,128]{2,1,0:T(4,128)S(1)} async-done(((f32[768,3,128]{2,1,0:T(4,128)}), f32[768,3,128]{2,1,0:T(4,128)S(1)}, u32[]{:S(2)}, u32[]{:S(2)}) %all-to-all-start.2) | async-done | bytes 1179680 | tf_op jit(solution)/shard_map/all_to_all | solution.py:96
  2531.1 52.1 %while.27 = (s32[]{:T(128)}, f32[96,2816]{1,0:T(8,128)S(1)}, s32[10]{0:T(128)S(1)}, f32[10,512,512]{2,1,0:T(8,128)}, s32[]{:T(128)}, /*index=5*/s32[]{:T(128)}, s32[]{:T(128)}) while((s32[]{:T(128)}, f32[96,2816]{1,0:T(8,128)S(1)}, s32[10]{0:T(128)S(1)}, f32[10,512,512]{2,1,0:T(8,128)}, s32[]{:T(128)}, /*index=5*/s32[]{:T(128)}, ...), condition=%wide.region_3.4_spmd, body=%wide.region_2.3_spmd.sunk | while | flops 301989888 | bytes 1835671 | solution.py:101
  2595.4 22.6 all-to-all-done.3
  (158 shorter events, 440.9 us)
Async XLA Ops:
  230.7 43.1 %copy-start.2 = (pred[6]{0:T(512)(128)(4,1)}, pred[6]{0:T(512)(128)(4,1)S(1)}, u32[]{:S(2)}) copy-start(pred[6]{0:T(512)(128)(4,1)S(1)} %get-tuple-element.236) | copy-start | bytes 22
  366.4 734.6 %all-to-all-start = ((f32[6,128,16384]{1,0,2:T(8,128)}), f32[6,128,16384]{1,0,2:T(8,128)}, u32[]{:S(2)}, u32[]{:S(2)}) async-start(f32[6,128,16384]{1,0,2:T(8,128)} %copy.74), calls=%async_computation | async-start | bytes 134217728 | tf_op jit(solution)/shard_map/all_to_all | solution.py:76
  379.4 103.5 %all-gather.2.cloned.1.call-start = ((), (), s32[]{:S(2)}) async-start(), calls=%async_computation.4 | async-start | bytes 11796480 | tf_op jit(solution)/shard_map/all_gather | solution.py:46
  1191.3 34.3 %copy-start = (s32[10]{0:T(128)S(1)}, s32[10]{0:T(128)}, u32[]{:S(2)}) copy-start(s32[10]{0:T(128)} %param.9) | copy-start | bytes 124
  1640.7 35.0 %copy-start.8 = (pred[24]{0:T(512)(128)(4,1)S(1)}, pred[24]{0:T(512)(128)(4,1)}, u32[]{:S(2)}) copy-start(pred[24]{0:T(512)(128)(4,1)} %get-tuple-element.233) | copy-start | bytes 76
  1640.7 35.0 %copy-start.9 = (pred[24]{0:T(512)(128)(4,1)S(1)}, pred[24]{0:T(512)(128)(4,1)}, u32[]{:S(2)}) copy-start(pred[24]{0:T(512)(128)(4,1)} %get-tuple-element.234) | copy-start | bytes 76
  1711.4 12.7 copy-start.4
  1711.4 25.9 copy-start.3
  1711.4 553.6 %all-to-all-start.1 = ((f32[24,128,4096]{2,1,0:T(8,128)}), f32[24,128,4096]{2,1,0:T(8,128)}, u32[]{:S(2)}, u32[]{:S(2)}) async-start(f32[24,128,4096]{2,1,0:T(8,128)} %select_select_fusion), calls=%async_computation.1 | async-start | bytes 100663296 | tf_op jit(solution)/shard_map/all_to_all | solution.py:83
  2298.1 7.8 slice-start.8
  2298.1 7.8 slice-start.9
  2305.9 4.8 slice-start.6
  2305.9 6.5 slice-start.7
  2310.7 6.0 slice-start.4
  2312.4 4.6 slice-start.5
  2316.7 5.1 slice-start.2
  2317.1 6.2 slice-start.3
  2321.9 5.6 slice-start
  2323.2 4.5 slice-start.1
  2437.0 48.2 %copy-start.5 = (pred[3]{0:T(512)(128)(4,1)S(1)}, pred[3]{0:T(512)(128)(4,1)}, u32[]{:S(2)}) copy-start(pred[3]{0:T(512)(128)(4,1)} %get-tuple-element.235) | copy-start | bytes 13
  2437.0 48.2 %copy-start.7 = (pred[3]{0:T(512)(128)(4,1)S(1)}, pred[3]{0:T(512)(128)(4,1)}, u32[]{:S(2)}) copy-start(pred[3]{0:T(512)(128)(4,1)} %get-tuple-element.197) | copy-start | bytes 13
  2483.2 47.9 %copy-start.1 = (s32[10]{0:T(128)S(1)}, s32[10]{0:T(128)}, u32[]{:S(2)}) copy-start(s32[10]{0:T(128)} %param.9) | copy-start | bytes 124
  2487.5 42.7 %all-to-all-start.2 = ((f32[768,3,128]{2,1,0:T(4,128)}), f32[768,3,128]{2,1,0:T(4,128)S(1)}, u32[]{:S(2)}, u32[]{:S(2)}) async-start(f32[768,3,128]{2,1,0:T(4,128)} %copy.85), calls=%async_computation.2 | async-start | bytes 3145728 | tf_op jit(solution)/shard_map/all_to_all | solution.py:96
  2531.0 57.8 %copy-start.6 = (s32[3]{0:T(128)S(1)}, s32[3]{0:T(128)}, u32[]{:S(2)}) copy-start(s32[3]{0:T(128)} %get-tuple-element.198) | copy-start | bytes 40
  2585.2 32.9 %all-to-all-start.3 = ((f32[96,24,128]{2,0,1:T(8,128)}), f32[96,24,128]{2,0,1:T(8,128)S(1)}, u32[]{:S(2)}, u32[]{:S(2)}) async-start(f32[96,24,128]{2,0,1:T(8,128)} %select_bitcast_fusion), calls=%async_computation.3 | async-start | bytes 2359296 | tf_op jit(solution)/shard_map/all_to_all | solution.py:108
Sparse Core Ops, SparseCore 0:
  381.8 101.0 all-gather.1
where the time goes:
time: 2690 us; the launch traced here: 2670 us
  waiting for transfers between devices  1300 us (48%)
  local copies, waits for them, and re-layouts  772 us (29%)
  other arithmetic  315 us (12%)
  matrix products  194 us (7%)
  starting transfers between devices  34.7 us (1%)
  between operations  33.2 us (1%)
    all_to_all x1, waiting for transfers between devices, body(): lax.all_to_all(picked, 'row', split_axis=2, concat_axis=0, tiled=True)  607 us
    all_to_all x1, waiting for transfers between devices, body(): lax.all_to_all(backsend, 'row', split_axis=0, concat_axis=2, tiled=True)  527 us
    dynamic_update_slice x10, local copies, waits for them, and re-layouts, left_step(): lax.dynamic_update_slice_in_dim(band_rows, result_rows, offset_row, 0)  222 us
    dot_general x10, matrix products, left_step(): jnp.dot(factor_now.T, window_rows, precision=lax.Precision.HIGHEST, prefe...  174 us
    unnamed x6, other arithmetic  133 us
    all_gather x1, waiting for transfers between devices, body(): all_factors = lax.all_gather(factors, 'col', axis=2, tiled=True)  102 us
    unnamed x43, local copies, waits for them, and re-layouts  78.5 us
    gather x5, local copies, waits for them, and re-layouts, body(): jnp.take(local_tiles, row_index, axis=0)  76.6 us
  transfers between devices with their start and end apart: 5, of which 5 were waited for; matrix products, arithmetic and copies ran while one was open for 1% of the time, Pallas kernels for 0%

commit v1 on v0

--- a/solution.py
+++ b/solution.py
@@ -73,7 +73,10 @@
     rows_each = -(-span_tiles // row_count)
     row_valid, row_index = pick_tiles(first_tile, rows_each, row_count, row_place, span_tiles)
     picked = jnp.where(row_valid[:, None, None], jnp.take(local_tiles, row_index, axis=0), 0.0)
-    received = lax.all_to_all(picked, "row", split_axis=2, concat_axis=0, tiled=True)
+    received = jnp.concatenate(
+        lax.all_to_all(jnp.stack(jnp.split(picked, lax.axis_size("row"), axis=2)), "row", 0, 0),
+        axis=0,
+    )
     band_rows = jnp.take(received, band_order(first_tile, row_count, rows_each, span_tiles), axis=0)
     band_rows = band_rows.reshape(span_tiles * tile_size, received.shape[2])
     band_rows = lax.fori_loop(0, WINS, left_step, band_rows)

time: 2690 us -> 2550 us (0.948)
  waiting for transfers between devices: 1300 us -> 1120 us
  other arithmetic: 315 us -> 348 us
    all_to_all x1, waiting for transfers between devices: 607 us -> 427 us  [body(): lax.all_to_all(jnp.stack(jnp.split(picked, lax.axis_size('row'), axis=2))...]
    slice x6 -> x7, local copies, waits for them, and re-layouts: 29.9 us -> 98.8 us  [body(): returned[member]]
    select_n x1 -> x0, local copies, waits for them, and re-layouts: 58.4 us -> none  [body(): jnp.where(row_valid[:, None, None], jnp.take(local_tiles, row_index, axis...]
    unnamed x43 -> x18, local copies, waits for them, and re-layouts: 78.5 us -> 41.7 us
    another operation x0 -> x1, other arithmetic: none -> 34.4 us  [body(): jnp.stack(jnp.split(picked, lax.axis_size('row'), axis=2))]
    another operation x0 -> x1, local copies, waits for them, and re-layouts: none -> 32.6 us  [body(): jnp.stack(jnp.split(picked, lax.axis_size('row'), axis=2))]
    unnamed x6 -> x1, other arithmetic: 133 us -> 133 us
where the time goes in v1:
time: 2550 us; the launch traced here: 2530 us
  waiting for transfers between devices  1120 us (44%)
  local copies, waits for them, and re-layouts  776 us (30%)
  other arithmetic  348 us (14%)
  matrix products  194 us (8%)
  between operations  33.9 us (1%)
  starting transfers between devices  33.6 us (1%)
  loops' own time  26.1 us (1%)
    all_to_all x1, waiting for transfers between devices, body(): lax.all_to_all(backsend, 'row', split_axis=0, concat_axis=2, tiled=True)  527 us
    all_to_all x1, waiting for transfers between devices, body(): lax.all_to_all(jnp.stack(jnp.split(picked, lax.axis_size('row'), axis=2))...  427 us
    dynamic_update_slice x10, local copies, waits for them, and re-layouts, left_step(): lax.dynamic_update_slice_in_dim(band_rows, result_rows, offset_row, 0)  222 us
    dot_general x10, matrix products, left_step(): jnp.dot(factor_now.T, window_rows, precision=lax.Precision.HIGHEST, prefe...  174 us
    unnamed x1, other arithmetic  133 us
    all_gather x1, waiting for transfers between devices, body(): all_factors = lax.all_gather(factors, 'col', axis=2, tiled=True)  103 us
    slice x7, local copies, waits for them, and re-layouts, body(): returned[member]  98.8 us
    gather x5, local copies, waits for them, and re-layouts, body(): jnp.take(local_tiles, row_index, axis=0)  76.6 us
  transfers between devices with their start and end apart: 5, of which 5 were waited for; matrix products, arithmetic and copies ran while one was open for 1% of the time, Pallas kernels for 0%

profile of v1, /device:TPU:2, one launch (start us, length us, event | category | flops | bytes accessed | tf_op | source)
XLA Modules:
  0.0 2528.5 jit_solution(3160413552058633533)
XLA Ops:
  9.8 133.4 %reduce.3 = f32[6,128,128,128]{3,2,1,0:T(8,128)} reduce(f32[6,1,128,128,1,128]{5,4,3,2,1,0:T(1,128)} %param.7, f32[]{:T(128)} %broadcast.1276), dimensions={1,4}, to_apply=%param.7.reduce_sub_computation.3 | reduce | bytes 100663296 | tf_op args[0]
  143.1 53.6 %reshape.636 = f32[6,128,16384]{2,1,0:T(8,128)} reshape(f32[6,128,128,128]{3,2,1,0:T(8,128)} %reduce.3) | data formatting | bytes 100663296 | tf_op jit(solution)/shard_map/reshape | solution.py:72
  196.7 22.2 fusion.50
  273.8 34.3 %fusion.10 = f32[6,128,16384]{2,1,0:T(8,128)} fusion(f32[6,128,5376]{2,1,0:T(8,128)} %gather_fusion.7, f32[6,128,5504]{2,1,0:T(8,128)} %gather_fusion.6, f32[6,128,5504]{2,1,0:T(8,128)} %gather_fusion.5, pred[6]{0:T(512)(128)(4,1)S(1)} %get-tuple-element.199, pred[6]{0:T(512)(128)(4,1)S(1)} %get-tuple-element.240), kind=kLoop, calls=%fused_computation.19 | loop fusion | flops 50331648 | bytes 100663312 | tf_op jit(solution)/shard_map/jit(_where)/select_n | solution.py:75
  308.1 32.6 %slice_bitcast_fusion.3 = (f32[1,6,128,4096]{3,2,1,0:T(8,128)}, f32[1,6,128,4096]{3,2,1,0:T(8,128)}, f32[1,6,128,4096]{3,2,1,0:T(8,128)}, f32[1,6,128,4096]{3,2,1,0:T(8,128)}) fusion(f32[6,128,16384]{2,1,0:T(8,128)} %fusion.10), kind=kLoop, calls=%fused_computation.27 | loop fusion | bytes 100663296 | tf_op jit(solution)/shard_map/stack | solution.py:77
  340.7 34.4 %pad_maximum_fusion = f32[4,6,128,4096]{3,2,1,0:T(8,128)} fusion(f32[1,6,128,4096]{3,2,1,0:T(8,128)} %get-tuple-element.212, f32[1,6,128,4096]{3,2,1,0:T(8,128)} %get-tuple-element.213, f32[1,6,128,4096]{3,2,1,0:T(8,128)} %get-tuple-element.214, f32[1,6,128,4096]{3,2,1,0:T(8,128)} %get-tuple-element.211), kind=kLoop, calls=%fused_computation.20 | loop fusion | flops 37748736 | bytes 100663296 | tf_op jit(solution)/shard_map/stack | solution.py:77
  387.8 102.5 %all-gather.2.cloned.1.call-done = f32[10,512,512]{1,2,0:T(8,128)} async-done(((f32[10,512,64]{1,2,0:T(8,128)}), f32[10,512,512]{1,2,0:T(8,128)}) %all-gather.2.cloned.1.call-update) | async-done | bytes 10485776 | tf_op jit(solution)/shard_map/all_gather | solution.py:46
  501.6 427.2 %all-to-all-done = f32[4,6,128,4096]{3,2,1,0:T(8,128)} async-done(((f32[4,6,128,4096]{3,2,1,0:T(8,128)}), f32[4,6,128,4096]{3,2,1,0:T(8,128)}, u32[]{:S(2)}, u32[]{:S(2)}) %all-to-all-start) | async-done | bytes 50331680 | tf_op jit(solution)/shard_map/all_to_all | solution.py:77
  928.8 32.3 %gather_fusion = f32[22,128,4096]{2,1,0:T(8,128)} fusion(f32[24,128,4096]{2,1,0:T(8,128)} %bitcast.12, s32[1024]{0:T(1024)S(1)} %pad_clamp_fusion.4), kind=kCustom, calls=%fused_computation | custom fusion | bytes 92274776 | tf_op jit(solution)/shard_map/jit(_take)/gather | solution.py:80
  961.0 34.3 %bitcast_select_fusion = f32[2816,4096]{1,0:T(8,128)} fusion(f32[22,128,4096]{2,1,0:T(8,128)} %gather_fusion, pred[2816]{0:T(1024)(128)(4,1)S(1)} %broadcast_bitcast_fusion.1), kind=kLoop, calls=%fused_computation.23 | loop fusion | flops 11534336 | bytes 92277504 | tf_op jit(solution)/shard_map/jit(_take)/select_n | solution.py:80
  995.3 414.5 %while.26 = (s32[]{:T(128)}, f32[2816,4096]{1,0:T(8,128)}, f32[10,512,512]{2,1,0:T(8,128)}, s32[10]{0:T(128)S(1)}, s32[]{:T(128)}, /*index=5*/s32[]{:T(128)}, s32[]{:T(128)}) while((s32[]{:T(128)}, f32[2816,4096]{1,0:T(8,128)}, f32[10,512,512]{2,1,0:T(8,128)}, s32[10]{0:T(128)S(1)}, s32[]{:T(128)}, /*index=5*/s32[]{:T(128)}, s32[]{:T(128)}) %tuple.99), condition=%wide.region_1.2_spmd, body=%wide.region_0.1_spmd.sunk | while | flops 12884901888 | bytes 34603672 | solution.py:82
  1014.5 22.2 dynamic_update_slice.27
  1056.0 22.2 dynamic_update_slice.27
  1080.2 17.4 fusion.68
  1097.6 22.2 dynamic_update_slice.27
  1139.1 22.3 dynamic_update_slice.27
  1180.6 22.3 dynamic_update_slice.27
  1222.1 22.3 dynamic_update_slice.27
  1263.6 22.2 dynamic_update_slice.27
  1305.1 22.2 dynamic_update_slice.27
  1346.6 22.3 dynamic_update_slice.27
  1388.2 21.7 dynamic_update_slice.27
  1409.8 35.0 %gather_fusion.1 = f32[24,128,4096]{2,1,0:T(8,128)} fusion(f32[22,128,4096]{2,1,0:T(8,128)} %bitcast.99, s32[1024]{0:T(1024)S(1)} %pad_clamp_fusion.3), kind=kCustom, calls=%fused_computation.1 | custom fusion | bytes 100663392 | tf_op jit(solution)/shard_map/jit(_take)/gather | solution.py:85
  1444.9 35.7 %select_select_fusion = f32[24,128,4096]{2,1,0:T(8,128)} fusion(f32[24,128,4096]{2,1,0:T(8,128)} %gather_fusion.1, pred[24]{0:T(512)(128)(4,1)S(1)} %get-tuple-element.237, pred[24]{0:T(512)(128)(4,1)S(1)} %get-tuple-element.238), kind=kLoop, calls=%fused_computation.22 | loop fusion | flops 25165824 | bytes 100663344 | tf_op jit(solution)/shard_map/jit(_where)/select_n | solution.py:85
  1506.9 527.0 %all-to-all-done.1 = f32[24,128,4096]{2,1,0:T(8,128)} async-done(((f32[24,128,4096]{2,1,0:T(8,128)}), f32[24,128,4096]{2,1,0:T(8,128)}, u32[]{:S(2)}, u32[]{:S(2)}) %all-to-all-start.1) | async-done | bytes 50331680 | tf_op jit(solution)/shard_map/all_to_all | solution.py:86
  2033.9 55.6 %copy.58 = f32[4,6,128,4096]{3,0,2,1:T(4,128)} copy(f32[4,6,128,4096]{3,2,1,0:T(8,128)} %bitcast.17) | data formatting | bytes 100663296 | tf_op jit(solution)/shard_map/all_to_all | solution.py:86
  2089.4 33.1 %fusion.49 = (f32[1,128,4,4096]{3,2,1,0:T(4,128)}, f32[1,128,4,4096]{3,2,1,0:T(4,128)}, f32[1,128,4,4096]{3,2,1,0:T(4,128)}, f32[1,128,4,4096]{3,2,1,0:T(4,128)}...) fusion(f32[6,128,4,4096]{3,2,1,0:T(4,128)} %bitcast.103), kind=kLoop, calls=%fused_computation.183 | loop fusion | bytes 100663296 | tf_op jit(solution)/shard_map/slice | solution.py:90
  2252.2 41.0 %copy.54 = f32[96,8,128,128]{3,2,1,0:T(8,128)} copy(f32[96,8,128,128]{3,1,2,0:T(8,128)} %bitcast.98) | data formatting | bytes 100663296
  2293.2 46.1 %copy.43 = f32[768,128,128]{2,0,1:T(8,128)} copy(f32[768,128,128]{2,1,0:T(8,128)} %bitcast.100) | data formatting | bytes 100663296 | tf_op jit(solution)/shard_map/reshape | solution.py:94
  2349.1 37.6 %all-to-all-done.2 = f32[768,3,128]{2,1,0:T(4,128)S(1)} async-done(((f32[768,3,128]{2,1,0:T(4,128)}), f32[768,3,128]{2,1,0:T(4,128)S(1)}, u32[]{:S(2)}, u32[]{:S(2)}) %all-to-all-start.2) | async-done | bytes 1179680 | tf_op jit(solution)/shard_map/all_to_all | solution.py:99
  2387.5 54.5 %while.27 = (s32[]{:T(128)}, f32[96,2816]{1,0:T(8,128)S(1)}, s32[10]{0:T(128)S(1)}, f32[10,512,512]{2,1,0:T(8,128)}, s32[]{:T(128)}, /*index=5*/s32[]{:T(128)}, s32[]{:T(128)}) while((s32[]{:T(128)}, f32[96,2816]{1,0:T(8,128)S(1)}, s32[10]{0:T(128)S(1)}, f32[10,512,512]{2,1,0:T(8,128)}, s32[]{:T(128)}, /*index=5*/s32[]{:T(128)}, ...), condition=%wide.region_3.4_spmd, body=%wide.region_2.3_spmd.sunk | while | flops 301989888 | bytes 1835671 | solution.py:104
  2454.9 22.0 all-to-all-done.3
  (130 shorter events, 489.4 us)
Async XLA Ops:
  230.7 43.2 %copy-start.2 = (pred[6]{0:T(512)(128)(4,1)}, pred[6]{0:T(512)(128)(4,1)S(1)}, u32[]{:S(2)}) copy-start(pred[6]{0:T(512)(128)(4,1)S(1)} %get-tuple-element.240) | copy-start | bytes 22
  375.1 553.6 %all-to-all-start = ((f32[4,6,128,4096]{3,2,1,0:T(8,128)}), f32[4,6,128,4096]{3,2,1,0:T(8,128)}, u32[]{:S(2)}, u32[]{:S(2)}) async-start(f32[4,6,128,4096]{3,2,1,0:T(8,128)} %pad_maximum_fusion), calls=%async_computation | async-start | bytes 100663296 | tf_op jit(solution)/shard_map/all_to_all | solution.py:77
  386.9 103.5 %all-gather.2.cloned.1.call-start = ((), (), s32[]{:S(2)}) async-start(), calls=%async_computation.4 | async-start | bytes 11796480 | tf_op jit(solution)/shard_map/all_gather | solution.py:46
  961.0 34.3 %copy-start = (s32[10]{0:T(128)S(1)}, s32[10]{0:T(128)}, u32[]{:S(2)}) copy-start(s32[10]{0:T(128)} %param.9) | copy-start | bytes 124
  1480.5 12.5 copy-start.4
  1480.5 25.7 %copy-start.3 = (pred[6]{0:T(512)(128)(4,1)S(1)}, pred[6]{0:T(512)(128)(4,1)}, u32[]{:S(2)}) copy-start(pred[6]{0:T(512)(128)(4,1)} %copy-done.2) | copy-start | bytes 22
  1480.5 553.4 %all-to-all-start.1 = ((f32[24,128,4096]{2,1,0:T(8,128)}), f32[24,128,4096]{2,1,0:T(8,128)}, u32[]{:S(2)}, u32[]{:S(2)}) async-start(f32[24,128,4096]{2,1,0:T(8,128)} %select_select_fusion), calls=%async_computation.1 | async-start | bytes 100663296 | tf_op jit(solution)/shard_map/all_to_all | solution.py:86
  2293.2 48.2 %copy-start.5 = (pred[3]{0:T(512)(128)(4,1)S(1)}, pred[3]{0:T(512)(128)(4,1)}, u32[]{:S(2)}) copy-start(pred[3]{0:T(512)(128)(4,1)} %get-tuple-element.239) | copy-start | bytes 13
  2293.2 48.2 %copy-start.7 = (pred[3]{0:T(512)(128)(4,1)S(1)}, pred[3]{0:T(512)(128)(4,1)}, u32[]{:S(2)}) copy-start(pred[3]{0:T(512)(128)(4,1)} %get-tuple-element.197) | copy-start | bytes 13
  2339.4 48.2 %copy-start.1 = (s32[10]{0:T(128)S(1)}, s32[10]{0:T(128)}, u32[]{:S(2)}) copy-start(s32[10]{0:T(128)} %param.9) | copy-start | bytes 124
  2343.7 43.0 %all-to-all-start.2 = ((f32[768,3,128]{2,1,0:T(4,128)}), f32[768,3,128]{2,1,0:T(4,128)S(1)}, u32[]{:S(2)}, u32[]{:S(2)}) async-start(f32[768,3,128]{2,1,0:T(4,128)} %copy.44), calls=%async_computation.2 | async-start | bytes 3145728 | tf_op jit(solution)/shard_map/all_to_all | solution.py:99
  2386.7 60.9 %copy-start.6 = (s32[3]{0:T(128)S(1)}, s32[3]{0:T(128)}, u32[]{:S(2)}) copy-start(s32[3]{0:T(128)} %get-tuple-element.198) | copy-start | bytes 40
  2444.1 32.9 %all-to-all-start.3 = ((f32[96,24,128]{2,0,1:T(8,128)}), f32[96,24,128]{2,0,1:T(8,128)S(1)}, u32[]{:S(2)}, u32[]{:S(2)}) async-start(f32[96,24,128]{2,0,1:T(8,128)} %select_bitcast_fusion), calls=%async_computation.3 | async-start | bytes 2359296 | tf_op jit(solution)/shard_map/all_to_all | solution.py:111
Sparse Core Ops, SparseCore 0:
  389.3 100.9 all-gather.1
